TPU v7x, 32 devices: a whole 2x2x4 slice. The times are simulated.
32 devices in a mesh: wide: 8 (over z, y), narrow: 4 (over x, core).
Axes of the slice: x: 2, y: 2, z: 4, core: 2. Of those that a mesh axis runs over, the one named last changes fastest.
Arguments:
- amplitudes: float32 [8, 512, 1024], P('wide', None, 'narrow'), may hold values from -6 to 6
- partner: float32 [64, 2048, 1024], P(None, 'wide', 'narrow'), may hold values from -0.1875 to 0.1875
- gate_block: float32 [8, 8], replicated, may hold values from -2 to 2
- slice_bits: int32 [6], replicated, may hold values from 0 to 1, as said below
- bit_order: int32 [9], replicated, may hold values from 0 to 8, each once
Outputs:
- contracted: float32 [8, 512, 2048], P(None, 'wide', 'narrow')
Inputs may be any that keep to these rules, and one draw needn't show every extreme that they name: bit_order is a permutation of 0 to 8. `slice_bits`: each entry is 0 or 1; the bits are never all equal.
All inputs are finite; a program needn't handle non-finite values.
Results may differ from a plain program's by a relative error of at most 0.00007.
Values sent between devices are 32-bit elements; how exact they have to be, the bound alone decides.
A program may use at most 64 MiB of HBM per device.

v0:
```python
import jax
import jax.numpy as jnp
from jax import lax
from jax.sharding import PartitionSpec as P


def source_rows(bit_order, total_rows):
    width = bit_order.shape[0]
    row_ids = jnp.arange(total_rows, dtype=jnp.int32)
    picked = jnp.bitwise_and(jnp.right_shift(row_ids[:, None], bit_order[None, :]), 1)
    powers = jnp.left_shift(jnp.ones((width,), jnp.int32), jnp.arange(width, dtype=jnp.int32))
    return jnp.sum(picked * powers[None, :], axis=1)


def slice_number(slice_bits):
    width = slice_bits.shape[0]
    powers = jnp.left_shift(jnp.ones((width,), jnp.int32), jnp.arange(width, dtype=jnp.int32))
    return jnp.sum(slice_bits * powers)


def contract_partner(left_rows, chosen):
    partial_terms = lax.dot_general(
        left_rows,
        lax.all_gather(chosen, "wide", axis=0, tiled=True),
        (((1,), (1,)), ((), ())),
        precision=lax.Precision.HIGHEST,
        preferred_element_type=jnp.float32,
    )
    return lax.psum_scatter(partial_terms, "narrow", scatter_dimension=1, tiled=True)


def gate_apply(gate_block, received):
    return jnp.einsum("qh,hlc->qlc", gate_block, received, precision=lax.Precision.HIGHEST)


def per_device(amplitudes, partner, gate_block, slice_bits, bit_order):
    source = source_rows(bit_order, amplitudes.shape[1])
    reordered = jnp.take(amplitudes[0], source, axis=0)
    chosen = lax.dynamic_index_in_dim(partner, slice_number(slice_bits), 0, keepdims=False)
    mixed = gate_apply(
        gate_block, lax.all_to_all(reordered[None], "wide", split_axis=1, concat_axis=0, tiled=True)
    )
    out_bits = mixed.shape[0]
    local_rows = mixed.shape[1]
    owned_part = contract_partner(mixed.reshape(out_bits * local_rows, mixed.shape[2]), chosen)
    return owned_part.reshape(out_bits, local_rows, owned_part.shape[1])


def solution(mesh):
    placed = (P("wide", None, "narrow"), P(None, "wide", "narrow"), P(), P(), P())
    return jax.shard_map(
        per_device, mesh=mesh, in_specs=placed, out_specs=P(None, "wide", "narrow"), check_vma=False
    )
```

profile of v0, /device:TPU:0, one launch (start us, length us, event | category | flops | bytes accessed | tf_op | source)
XLA Modules:
  0.0 127.9 jit_solution(4080367930417074534)
XLA Ops:
  6.5 0.0 copy-start
  6.5 0.0 all-gather.3.cloned.1.call-start
  6.5 1.4 %multiply_reduce_fusion.1 = s32[]{:T(128)} fusion(s32[6]{0:T(128)} %param.8), kind=kLoop, calls=%fused_computation.12 | loop fusion | flops 17 | bytes 28 | tf_op jit(solution)/shard_map/reduce_sum | solution.py:18
  9.8 1.7 %constant_dynamic-slice_fusion = f32[1,256,256]{2,1,0:T(8,128)} fusion(f32[64,256,256]{2,1,0:T(8,128)} %param.6, s32[]{:T(128)S(6)} %select_n.34), kind=kLoop, calls=%fused_computation.14 | loop fusion | bytes 524292 | tf_op jit(solution)/shard_map/jit(dynamic_index_in_dim)/dynamic_slice | solution.py:39
  11.5 0.0 all-gather.3.cloned.1.call-update
  11.5 0.0 reduce-scatter.2.cloned.1.call-start
  11.6 0.7 multiply_reduce_fusion
  12.4 0.0 copy-done
  12.4 0.0 copy-start.1
  12.4 1.6 %gather_fusion = f32[512,256]{1,0:T(8,128)S(1)} fusion(f32[512,256]{1,0:T(8,128)S(1)} %bitcast.17, s32[1024]{0:T(1024)S(1)} %pad_clamp_fusion), kind=kCustom, calls=%fused_computation | custom fusion | bytes 1050624 | tf_op jit(solution)/shard_map/jit(_take)/gather | solution.py:38
  14.0 0.1 bitcast_select_fusion
  14.1 0.5 copy.11
  14.7 30.0 %all_to_all.12 = f32[1,512,256]{2,0,1:T(1,128)S(1)} all-to-all(f32[1,512,256]{2,0,1:T(1,128)S(1)} %copy.11), channel_id=1, replica_groups=mesh['wide'=8,'narrow'=4] {'wide'}, dimensions={1} | all-to-all | bytes 1048576 | tf_op jit(solution)/shard_map/all_to_all | solution.py:41
  44.7 0.0 copy-done.1
  44.8 0.9 convolution_bitcast_fusion
  45.6 0.2 copy.13
  45.8 25.3 %all-gather.3.cloned.1.call-done = f32[1,2048,256]{2,1,0:T(8,128)} async-done(((f32[1,256,256]{2,1,0:T(8,128)}), f32[1,2048,256]{2,1,0:T(8,128)}) %all-gather.3.cloned.1.call-update) | async-done | bytes 2097168 | tf_op jit(solution)/shard_map/all_gather | solution.py:24
  71.1 6.7 %fusion = f32[512,2048]{1,0:T(8,128)} fusion(f32[512,256]{1,0:T(8,128)S(1)} %bitcast.19, f32[1,2048,256]{2,1,0:T(8,128)} %all-gather.3.cloned.1.call-done), kind=kOutput, calls=%fused_computation.1 | convolution fusion | flops 3221225472 | bytes 6815744 | tf_op jit(solution)/shard_map/dot_general | solution.py:22
  77.8 0.0 reduce-scatter.2.cloned.1.call-update
  77.9 43.2 %reduce-scatter.2.cloned.1.call-done = f32[512,512]{1,0:T(8,128)} async-done(((f32[512,2048]{1,0:T(8,128)}), f32[512,512]{1,0:T(8,128)}) %reduce-scatter.2.cloned.1.call-update) | async-done | bytes 1048592 | tf_op jit(solution)/shard_map/reduce_scatter | solution.py:29
  (5 shorter events, 0.1 us)
Async XLA Ops:
  6.5 5.8 %copy-start = (f32[1,512,256]{2,1,0:T(8,128)S(1)}, f32[1,512,256]{2,1,0:T(8,128)}, u32[]{:S(2)}) copy-start(f32[1,512,256]{2,1,0:T(8,128)} %param.5) | copy-start | bytes 1572868
  6.5 64.5 %all-gather.3.cloned.1.call-start = ((), (), s32[]{:S(2)}) async-start(), calls=%async_computation.3 | async-start | bytes 2359296 | tf_op jit(solution)/shard_map/all_gather | solution.py:24
  11.5 109.5 %reduce-scatter.2.cloned.1.call-start = ((), (), s32[]{:S(2)}) async-start(), calls=%async_computation.2 | async-start | bytes 5242880 | tf_op jit(solution)/shard_map/reduce_scatter | solution.py:29
  12.4 32.4 %copy-start.1 = (f32[8,8]{1,0:T(8,128)S(1)}, f32[8,8]{1,0:T(8,128)}, u32[]{:S(2)}) copy-start(f32[8,8]{1,0:T(8,128)} %param.7) | copy-start | bytes 772
Sparse Core Ops, SparseCore 0:
  11.7 59.3 all-gather.2
  78.0 43.0 reduce-scatter.1
where the time goes:
time: 128 us
  waiting for transfers between devices  68.5 us (54%)
  blocking collectives  30 us (23%)
  between operations  15.4 us (12%)
  matrix products  7.63 us (6%)
  local copies, waits for them, and re-layouts  4 us (3%)
  other arithmetic  2.26 us (2%)
    reduce_scatter x1, waiting for transfers between devices, contract_partner(): lax.psum_scatter(partial_terms, 'narrow', scatter_dimension=1, tiled=True)  43.2 us
    all_to_all x1, blocking collectives, per_device(): lax.all_to_all(reordered[None], 'wide', split_axis=1, concat_axis=0, tile...  30 us
    all_gather x1, waiting for transfers between devices, contract_partner(): lax.all_gather(chosen, 'wide', axis=0, tiled=True)  25.3 us
    dot_general x1, matrix products, contract_partner(): lax.dot_general(left_rows, lax.all_gather(chosen, 'wide', axis=0, tiled=T...  6.75 us
  transfers between devices with their start and end apart: 2, of which 2 were waited for; matrix products, arithmetic and copies ran while one was open for 3% of the time, Pallas kernels for 0%

commit v1 on v0

--- a/solution.py
+++ b/solution.py
@@ -2,6 +2,27 @@
 import jax.numpy as jnp
 from jax import lax
 from jax.sharding import PartitionSpec as P
+
+
+def ring_gather(x, axis, dim):
+    peers, index, width = (lax.axis_size(axis), lax.axis_index(axis), x.shape[dim])
+    right = [(i, (i + 1) % peers) for i in range(peers)]
+    backward = [(i, (i - 1) % peers) for i in range(peers)]
+    out = jnp.zeros((*x.shape[:dim], peers * width, *x.shape[dim + 1 :]), x.dtype)
+    out = lax.dynamic_update_slice_in_dim(out, x, index * width, axis=dim)
+    from_left = from_right = x
+    halfway = peers // 2
+    for step in range(1, halfway + 1):
+        from_left = lax.ppermute(from_left, axis, right)
+        out = lax.dynamic_update_slice_in_dim(
+            out, from_left, (index - step) % peers * width, axis=dim
+        )
+        if step < peers - halfway:
+            from_right = lax.ppermute(from_right, axis, backward)
+            out = lax.dynamic_update_slice_in_dim(
+                out, from_right, (index + step) % peers * width, axis=dim
+            )
+    return out
 
 
 def source_rows(bit_order, total_rows):
@@ -21,7 +42,7 @@
 def contract_partner(left_rows, chosen):
     partial_terms = lax.dot_general(
         left_rows,
-        lax.all_gather(chosen, "wide", axis=0, tiled=True),
+        ring_gather(chosen, "wide", 0),
         (((1,), (1,)), ((), ())),
         precision=lax.Precision.HIGHEST,
         preferred_element_type=jnp.float32,

time: 128 us -> 123 us (0.961)
  blocking collectives: 30 us -> 0 us
  starting transfers between devices: 0.04 us -> 23.9 us
  local copies, waits for them, and re-layouts: 4 us -> 8.95 us
  matrix products: 7.63 us -> 6.02 us
  waiting for transfers between devices: 68.5 us -> 66.9 us
    all_to_all x1 -> x0, blocking collectives: 30 us -> none  [per_device(): lax.all_to_all(reordered[None], 'wide', split_axis=1, concat_axis=0, tile...]
    all_gather x1 -> x0, waiting for transfers between devices: 25.3 us -> none  [contract_partner(): lax.all_gather(chosen, 'wide', axis=0, tiled=True)]
    ppermute x0 -> x7, waiting for transfers between devices: none -> 23.5 us  [the longest x4 23.5 us: ring_gather(): from_left = lax.ppermute(from_left, axis, right)]
    ppermute x0 -> x7, starting transfers between devices: none -> 20.3 us  [the longest x4 11 us: ring_gather(): from_left = lax.ppermute(from_left, axis, right)]
    dynamic_update_slice x0 -> x8, local copies, waits for them, and re-layouts: none -> 5.69 us  [the longest x4 2.97 us: ring_gather(): lax.dynamic_update_slice_in_dim(out, from_left, (index - step) % peers *...]
    all_to_all x0 -> x1, starting transfers between devices: none -> 3.49 us  [per_device(): lax.all_to_all(reordered[None], 'wide', split_axis=1, concat_axis=0, tile...]
    dynamic_slice x1 -> x0, local copies, waits for them, and re-layouts: 1.67 us -> none  [per_device(): lax.dynamic_index_in_dim(partner, slice_number(slice_bits), 0, keepdims=F...]
    dot_general x1, matrix products: 6.75 us -> 5.13 us  [contract_partner(): lax.dot_general(left_rows, ring_gather(chosen, 'wide', 0), (((1,), (1,)),...]
  transfers between devices with their start and end apart: 2 -> 9, of which waited for: 2 -> 5; matrix products, arithmetic and copies ran while one was open for 3% -> 7% of each run, Pallas kernels for 0% -> 0%
where the time goes in v1:
time: 123 us
  waiting for transfers between devices  66.9 us (54%)
  starting transfers between devices  23.9 us (19%)
  between operations  15.5 us (13%)
  local copies, waits for them, and re-layouts  8.95 us (7%)
  matrix products  6.02 us (5%)
  other arithmetic  1.61 us (1%)
    reduce_scatter x1, waiting for transfers between devices, contract_partner(): lax.psum_scatter(partial_terms, 'narrow', scatter_dimension=1, tiled=True)  43.4 us
    ppermute x4, waiting for transfers between devices, ring_gather(): from_left = lax.ppermute(from_left, axis, right)  23.5 us
    ppermute x4, starting transfers between devices, ring_gather(): from_left = lax.ppermute(from_left, axis, right)  11 us
    ppermute x3, starting transfers between devices, ring_gather(): from_right = lax.ppermute(from_right, axis, backward)  9.37 us
    dot_general x1, matrix products, contract_partner(): lax.dot_general(left_rows, ring_gather(chosen, 'wide', 0), (((1,), (1,)),...  5.13 us
    all_to_all x1, starting transfers between devices, per_device(): lax.all_to_all(reordered[None], 'wide', split_axis=1, concat_axis=0, tile...  3.49 us
    dynamic_update_slice x4, local copies, waits for them, and re-layouts, ring_gather(): lax.dynamic_update_slice_in_dim(out, from_left, (index - step) % peers *...  2.97 us
  transfers between devices with their start and end apart: 9, of which 5 were waited for; matrix products, arithmetic and copies ran while one was open for 7% of the time, Pallas kernels for 0%

profile of v1, /device:TPU:0, one launch (start us, length us, event | category | flops | bytes accessed | tf_op | source)
XLA Modules:
  0.0 122.9 jit_solution(12099227773220351822)
XLA Ops:
  6.5 1.4 %multiply_reduce_fusion.1 = s32[]{:T(128)} fusion(s32[6]{0:T(128)} %param.8), kind=kLoop, calls=%fused_computation.19 | loop fusion | flops 17 | bytes 28 | tf_op jit(solution)/shard_map/reduce_sum | solution.py:39
  10.0 1.7 %constant_dynamic-update-slice_fusion.7 = (f32[2048,256]{1,0:T(8,128)S(1)}, f32[256,256]{1,0:T(8,128)}) fusion(f32[2048,256]{1,0:T(8,128)S(1)} %broadcast_in_dim.19, s32[]{:T(128)S(6)} %select_n.90, f32[64,256,256]{2,1,0:T(8,128)} %param.6, s32[]{:T(128)S(6)} %select_n.89), kind=kLoop, calls=%fused_computation.17 | loop fusion | bytes 786440 | tf_op jit(solution)/shard_map/dynamic_update_slice | solution.py:12
  11.7 3.0 %collective-permute-start = (f32[256,256]{1,0:T(8,128)}, f32[256,256]{1,0:T(8,128)}, u32[]{:S(2)}, u32[]{:S(2)}) collective-permute-start(f32[256,256]{1,0:T(8,128)} %get-tuple-element.6), channel_id=1, source_target_pairs={{0,4},{4,8},{8,12},{12,16},{16,20},{20,24},{24,28},{28,0},{1,5},{5... | collective-permute-start | bytes 786440 | tf_op jit(solution)/shard_map/ppermute | solution.py:16
  14.7 3.0 %collective-permute-start.1 = (f32[256,256]{1,0:T(8,128)}, f32[256,256]{1,0:T(8,128)S(1)}, u32[]{:S(2)}, u32[]{:S(2)}) collective-permute-start(f32[256,256]{1,0:T(8,128)} %get-tuple-element.6), channel_id=1, source_target_pairs={{0,28},{4,0},{8,4},{12,8},{16,12},{20,16},{24,20},{28,24},{1,29},{... | collective-permute-start | bytes 786440 | tf_op jit(solution)/shard_map/ppermute | solution.py:21
  17.8 1.6 %gather_fusion = f32[512,256]{1,0:T(8,128)S(1)} fusion(f32[512,256]{1,0:T(8,128)S(1)} %bitcast.18, s32[1024]{0:T(1024)S(1)} %pad_clamp_fusion), kind=kCustom, calls=%fused_computation | custom fusion | bytes 1050624 | tf_op jit(solution)/shard_map/jit(_take)/gather | solution.py:59
  19.6 1.3 %copy.11 = f32[1,512,256]{2,0,1:T(1,128)} copy(f32[1,512,256]{2,1,0:T(8,128)S(1)} %bitcast_select_fusion) | data formatting | bytes 1048576 | tf_op jit(solution)/shard_map/jit(_take)/select_n | solution.py:59
  20.9 3.5 %all-to-all-start = ((f32[1,512,256]{2,0,1:T(1,128)}), f32[1,512,256]{2,0,1:T(1,128)S(1)}, u32[]{:S(2)}, u32[]{:S(2)}) async-start(f32[1,512,256]{2,0,1:T(1,128)} %copy.11), calls=%async_computation | async-start | bytes 1048576 | tf_op jit(solution)/shard_map/all_to_all | solution.py:62
  24.4 3.9 %collective-permute-done = f32[256,256]{1,0:T(8,128)} collective-permute-done((f32[256,256]{1,0:T(8,128)}, f32[256,256]{1,0:T(8,128)}, u32[]{:S(2)}, u32[]{:S(2)}) %collective-permute-start) | collective-permute-done | bytes 262176 | tf_op jit(solution)/shard_map/ppermute | solution.py:16
  28.3 3.7 %collective-permute-start.2 = (f32[256,256]{1,0:T(8,128)}, f32[256,256]{1,0:T(8,128)}, u32[]{:S(2)}, u32[]{:S(2)}) collective-permute-start(f32[256,256]{1,0:T(8,128)} %collective-permute-done), channel_id=1, source_target_pairs={{0,4},{4,8},{8,12},{12,16},{16,20},{20,24},{24,28},{28,0},{1,5},{5... | collective-permute-start | bytes 786440 | tf_op jit(solution)/shard_map/ppermute | solution.py:16
  32.0 3.2 %collective-permute-start.3 = (f32[256,256]{1,0:T(8,128)S(1)}, f32[256,256]{1,0:T(8,128)}, u32[]{:S(2)}, u32[]{:S(2)}) collective-permute-start(f32[256,256]{1,0:T(8,128)S(1)} %collective-permute-done.1), channel_id=1, source_target_pairs={{0,28},{4,0},{8,4},{12,8},{16,12},{20,16},{24,20},{28,24},{1,29},{... | collective-permute-start | bytes 786440 | tf_op jit(solution)/shard_map/ppermute | solution.py:21
  35.3 1.0 constant_dynamic-update-slice_fusion.6
  36.3 7.4 %collective-permute-done.2 = f32[256,256]{1,0:T(8,128)} collective-permute-done((f32[256,256]{1,0:T(8,128)}, f32[256,256]{1,0:T(8,128)}, u32[]{:S(2)}, u32[]{:S(2)}) %collective-permute-start.2) | collective-permute-done | bytes 262176 | tf_op jit(solution)/shard_map/ppermute | solution.py:16
  43.7 1.8 %collective-permute-start.4 = (f32[256,256]{1,0:T(8,128)}, f32[256,256]{1,0:T(8,128)}, u32[]{:S(2)}, u32[]{:S(2)}) collective-permute-start(f32[256,256]{1,0:T(8,128)} %collective-permute-done.2), channel_id=1, source_target_pairs={{0,4},{4,8},{8,12},{12,16},{16,20},{20,24},{24,28},{28,0},{1,5},{5... | collective-permute-start | bytes 786440 | tf_op jit(solution)/shard_map/ppermute | solution.py:16
  45.5 3.1 %collective-permute-start.5 = (f32[256,256]{1,0:T(8,128)}, f32[256,256]{1,0:T(8,128)S(1)}, u32[]{:S(2)}, u32[]{:S(2)}) collective-permute-start(f32[256,256]{1,0:T(8,128)} %collective-permute-done.3), channel_id=1, source_target_pairs={{0,28},{4,0},{8,4},{12,8},{16,12},{20,16},{24,20},{28,24},{1,29},{... | collective-permute-start | bytes 786440 | tf_op jit(solution)/shard_map/ppermute | solution.py:21
  48.6 1.0 constant_dynamic-update-slice_fusion.4
  49.6 1.0 constant_dynamic-update-slice_fusion.3
  50.6 5.8 %collective-permute-done.4 = f32[256,256]{1,0:T(8,128)} collective-permute-done((f32[256,256]{1,0:T(8,128)}, f32[256,256]{1,0:T(8,128)}, u32[]{:S(2)}, u32[]{:S(2)}) %collective-permute-start.4) | collective-permute-done | bytes 262176 | tf_op jit(solution)/shard_map/ppermute | solution.py:16
  56.3 2.5 %collective-permute-start.6 = (f32[256,256]{1,0:T(8,128)}, f32[256,256]{1,0:T(8,128)S(1)}, u32[]{:S(2)}, u32[]{:S(2)}) collective-permute-start(f32[256,256]{1,0:T(8,128)} %collective-permute-done.4), channel_id=1, source_target_pairs={{0,4},{4,8},{8,12},{12,16},{16,20},{20,24},{24,28},{28,0},{1,5},{5... | collective-permute-start | bytes 786440 | tf_op jit(solution)/shard_map/ppermute | solution.py:16
  58.8 1.0 constant_dynamic-update-slice_fusion.2
  59.9 0.9 convolution_bitcast_fusion
  60.8 0.2 copy.13
  61.0 6.5 %collective-permute-done.6 = f32[256,256]{1,0:T(8,128)S(1)} collective-permute-done((f32[256,256]{1,0:T(8,128)}, f32[256,256]{1,0:T(8,128)S(1)}, u32[]{:S(2)}, u32[]{:S(2)}) %collective-permute-start.6) | collective-permute-done | bytes 262176 | tf_op jit(solution)/shard_map/ppermute | solution.py:16
  67.5 5.1 %fusion.2 = f32[512,2048]{1,0:T(8,128)} fusion(f32[512,256]{1,0:T(8,128)S(1)} %bitcast.20, f32[2048,256]{1,0:T(8,128)S(1)} %constant_dynamic-update-slice_fusion), kind=kOutput, calls=%fused_computation.21 | convolution fusion | flops 3221225472 | bytes 6815744 | tf_op jit(solution)/shard_map/dot_general | solution.py:43
  72.7 43.4 %reduce-scatter.2.cloned.1.call-done = f32[512,512]{1,0:T(8,128)} async-done(((f32[512,2048]{1,0:T(8,128)}), f32[512,512]{1,0:T(8,128)}) %reduce-scatter.2.cloned.1.call-update) | async-done | bytes 1048592 | tf_op jit(solution)/shard_map/reduce_scatter | solution.py:50
  (23 shorter events, 0.6 us)
Async XLA Ops:
  6.5 11.3 %copy-start = (f32[1,512,256]{2,1,0:T(8,128)S(1)}, f32[1,512,256]{2,1,0:T(8,128)}, u32[]{:S(2)}) copy-start(f32[1,512,256]{2,1,0:T(8,128)} %param.5) | copy-start | bytes 1572868
  6.5 11.2 %copy-start.2 = (s32[9]{0:T(128)S(1)}, s32[9]{0:T(128)}, u32[]{:S(2)}) copy-start(s32[9]{0:T(128)} %param.9) | copy-start | bytes 112
  11.7 16.6 %collective-permute-start = (f32[256,256]{1,0:T(8,128)}, f32[256,256]{1,0:T(8,128)}, u32[]{:S(2)}, u32[]{:S(2)}) collective-permute-start(f32[256,256]{1,0:T(8,128)} %get-tuple-element.6), channel_id=1, source_target_pairs={{0,4},{4,8},{8,12},{12,16},{16,20},{20,24},{24,28},{28,0},{1,5},{5... | collective-permute-start | bytes 786440 | tf_op jit(solution)/shard_map/ppermute | solution.py:16
  14.7 17.4 %collective-permute-start.1 = (f32[256,256]{1,0:T(8,128)}, f32[256,256]{1,0:T(8,128)S(1)}, u32[]{:S(2)}, u32[]{:S(2)}) collective-permute-start(f32[256,256]{1,0:T(8,128)} %get-tuple-element.6), channel_id=1, source_target_pairs={{0,28},{4,0},{8,4},{12,8},{16,12},{20,16},{24,20},{28,24},{1,29},{... | collective-permute-start | bytes 786440 | tf_op jit(solution)/shard_map/ppermute | solution.py:21
  20.9 39.0 %all-to-all-start = ((f32[1,512,256]{2,0,1:T(1,128)}), f32[1,512,256]{2,0,1:T(1,128)S(1)}, u32[]{:S(2)}, u32[]{:S(2)}) async-start(f32[1,512,256]{2,0,1:T(1,128)} %copy.11), calls=%async_computation | async-start | bytes 1048576 | tf_op jit(solution)/shard_map/all_to_all | solution.py:62
  24.4 91.6 %reduce-scatter.2.cloned.1.call-start = ((), (), s32[]{:S(2)}) async-start(), calls=%async_computation.2 | async-start | bytes 5242880 | tf_op jit(solution)/shard_map/reduce_scatter | solution.py:50
  28.3 15.4 %collective-permute-start.2 = (f32[256,256]{1,0:T(8,128)}, f32[256,256]{1,0:T(8,128)}, u32[]{:S(2)}, u32[]{:S(2)}) collective-permute-start(f32[256,256]{1,0:T(8,128)} %collective-permute-done), channel_id=1, source_target_pairs={{0,4},{4,8},{8,12},{12,16},{16,20},{20,24},{24,28},{28,0},{1,5},{5... | collective-permute-start | bytes 786440 | tf_op jit(solution)/shard_map/ppermute | solution.py:16
  32.0 13.5 %collective-permute-start.3 = (f32[256,256]{1,0:T(8,128)S(1)}, f32[256,256]{1,0:T(8,128)}, u32[]{:S(2)}, u32[]{:S(2)}) collective-permute-start(f32[256,256]{1,0:T(8,128)S(1)} %collective-permute-done.1), channel_id=1, source_target_pairs={{0,28},{4,0},{8,4},{12,8},{16,12},{20,16},{24,20},{28,24},{1,29},{... | collective-permute-start | bytes 786440 | tf_op jit(solution)/shard_map/ppermute | solution.py:21
  35.3 24.6 %copy-start.1 = (f32[8,8]{1,0:T(8,128)S(1)}, f32[8,8]{1,0:T(8,128)}, u32[]{:S(2)}) copy-start(f32[8,8]{1,0:T(8,128)} %param.7) | copy-start | bytes 772
  43.7 12.6 %collective-permute-start.4 = (f32[256,256]{1,0:T(8,128)}, f32[256,256]{1,0:T(8,128)}, u32[]{:S(2)}, u32[]{:S(2)}) collective-permute-start(f32[256,256]{1,0:T(8,128)} %collective-permute-done.2), channel_id=1, source_target_pairs={{0,4},{4,8},{8,12},{12,16},{16,20},{20,24},{24,28},{28,0},{1,5},{5... | collective-permute-start | bytes 786440 | tf_op jit(solution)/shard_map/ppermute | solution.py:16
  45.5 14.3 %collective-permute-start.5 = (f32[256,256]{1,0:T(8,128)}, f32[256,256]{1,0:T(8,128)S(1)}, u32[]{:S(2)}, u32[]{:S(2)}) collective-permute-start(f32[256,256]{1,0:T(8,128)} %collective-permute-done.3), channel_id=1, source_target_pairs={{0,28},{4,0},{8,4},{12,8},{16,12},{20,16},{24,20},{28,24},{1,29},{... | collective-permute-start | bytes 786440 | tf_op jit(solution)/shard_map/ppermute | solution.py:21
  56.3 11.1 %collective-permute-start.6 = (f32[256,256]{1,0:T(8,128)}, f32[256,256]{1,0:T(8,128)S(1)}, u32[]{:S(2)}, u32[]{:S(2)}) collective-permute-start(f32[256,256]{1,0:T(8,128)} %collective-permute-done.4), channel_id=1, source_target_pairs={{0,4},{4,8},{8,12},{12,16},{16,20},{20,24},{24,28},{28,0},{1,5},{5... | collective-permute-start | bytes 786440 | tf_op jit(solution)/shard_map/ppermute | solution.py:16
Sparse Core Ops, SparseCore 0:
  72.8 43.2 reduce-scatter.1
